TPU v7x, 32 devices: a whole 2x2x4 slice. The times are simulated.
32 devices in a mesh: dp: 8 (over y, x, core), tensor: 4 (over z).
Axes of the slice: x: 2, y: 2, z: 4, core: 2. Of those that a mesh axis runs over, the one named last changes fastest.
Arguments:
- inputs: bfloat16 [6144, 2048], P('dp'), may hold values from -6 to 6
- block_ids: int32 [8, 768], P('dp'), may hold values from 0 to 3, never falling along the last dimension, each value on 1 to 256 neighbouring positions
- first_gain: float32 [2048], replicated, may hold values from 0.5 to 1.5
- first_shift: float32 [2048], replicated, may hold values from -3 to 3
- mixing_weight: bfloat16 [2048, 3, 2048], P(None, None, 'tensor'), may hold values from -0.125 to 0.125
- mixing_bias: float32 [2, 2048], P(None, 'tensor'), may hold values from -3 to 3
- output_weight: bfloat16 [2048, 2048], P('tensor'), may hold values from -0.75 to 0.75
- output_bias: float32 [2048], replicated, may hold values from -3 to 3
- second_gain: float32 [2048], replicated, may hold values from 0.5 to 1.5
- second_shift: float32 [2048], replicated, may hold values from -3 to 3
- expand_weight: bfloat16 [2048, 8192], P(None, 'tensor'), may hold values from -0.125 to 0.125
- expand_bias: float32 [8192], P('tensor'), may hold values from -3 to 3
- shrink_weight: bfloat16 [8192, 2048], P('tensor'), may hold values from -0.0625 to 0.0625
- shrink_bias: float32 [2048], replicated, may hold values from -3 to 3
- cotangent: bfloat16 [6144, 2048], P('dp'), may hold values from -6 to 6
Outputs:
- outputs: bfloat16 [6144, 2048], P('dp')
- input_grad: bfloat16 [6144, 2048], P('dp')
- first_gain_grad: float32 [2048], replicated
- first_shift_grad: float32 [2048], replicated
- mixing_weight_grad: float32 [2048, 3, 2048], P(None, None, 'tensor')
- mixing_bias_grad: float32 [2, 2048], P(None, 'tensor')
- output_weight_grad: float32 [2048, 2048], P('tensor')
- output_bias_grad: float32 [2048], replicated
- second_gain_grad: float32 [2048], replicated
- second_shift_grad: float32 [2048], replicated
- expand_weight_grad: float32 [2048, 8192], P(None, 'tensor')
- expand_bias_grad: float32 [8192], P('tensor')
- shrink_weight_grad: float32 [8192, 2048], P('tensor')
- shrink_bias_grad: float32 [2048], replicated
Inputs may be any that keep to these rules, and one draw needn't show every extreme that they name: `block_ids`: each sequence's block numbers start at 0, never fall, rise by one from block to block, give 4 blocks of 1 to 256 tokens, and one block has exactly 256 tokens.
All inputs are finite; a program needn't handle non-finite values.
Results may differ from a plain program's by a relative error of at most 0.014.
Values may be sent and summed in bfloat16 or wider, within the bound.
A program may use at most 256 MiB of HBM per device.

v0:
```python
import math
import jax
import jax.numpy as jnp
from jax import lax
from jax.sharding import PartitionSpec as P

H = 32
HD = 64
EPS = 1e-05


def layer_norm(values, scale_gain, shift_bias):
    row_mean = jnp.mean(values, axis=-1, keepdims=True)
    centred = values - row_mean
    row_var = jnp.mean(centred * centred, axis=-1, keepdims=True)
    return centred * lax.rsqrt(row_var + EPS) * scale_gain + shift_bias


def norm_backward(values, scale_gain, shift_bias, upstream):
    _, pull_back = jax.vjp(layer_norm, values, scale_gain, shift_bias)
    return pull_back(upstream)


def gelu_exact(values):
    return jax.nn.gelu(values, approximate=False)


def biased_scores(query, keys, blocks, first_head):
    length, local_heads, head_width = query.shape
    scores = jnp.einsum("qhd,khd->hqk", query, keys, preferred_element_type=jnp.float32) * (
        1.0 / math.sqrt(head_width)
    )
    heads_index = (first_head + jnp.arange(local_heads)).astype(jnp.float32)
    slopes = 2.0 ** (-8.0 * (heads_index + 1.0) / H)
    places = jnp.arange(length)
    offsets = (places[None, :] - places[:, None]).astype(jnp.float32)
    scores = scores + slopes[:, None, None] * offsets[None]
    allowed = blocks[None, :] <= blocks[:, None]
    return jnp.where(allowed[None], scores, -1e30)


def on_device(
    inputs,
    block_ids,
    first_gain,
    first_shift,
    mixing_weight,
    mixing_bias,
    output_weight,
    output_bias,
    second_gain,
    second_shift,
    expand_weight,
    expand_bias,
    shrink_weight,
    shrink_bias,
    cotangent,
):
    source = inputs.astype(jnp.float32)
    upstream = cotangent.astype(jnp.float32)
    length, width = source.shape
    blocks = block_ids[0]
    local_width = mixing_weight.shape[2]
    local_heads = local_width // HD
    first_head = lax.axis_index("tensor") * local_heads
    normed_low = layer_norm(source, first_gain, first_shift).astype(jnp.bfloat16)
    flat_weight = mixing_weight.reshape(width, 3 * local_width)
    mixed = jnp.dot(normed_low, flat_weight, preferred_element_type=jnp.float32).reshape(
        length, 3, local_width
    )
    query = (mixed[:, 0] + mixing_bias[0]).astype(jnp.bfloat16).reshape(length, local_heads, HD)
    keys = mixed[:, 1].astype(jnp.bfloat16).reshape(length, local_heads, HD)
    vals = (mixed[:, 2] + mixing_bias[1]).astype(jnp.bfloat16).reshape(length, local_heads, HD)
    masked = biased_scores(query, keys, blocks, first_head)
    row_top = jnp.max(masked, axis=-1, keepdims=True)
    logsum = row_top + jnp.log(jnp.sum(jnp.exp(masked - row_top), axis=-1, keepdims=True))
    probs_low = jnp.exp(masked - logsum).astype(jnp.bfloat16)
    attended = (
        jnp.einsum("hqk,khd->qhd", probs_low, vals, preferred_element_type=jnp.float32)
        .reshape(length, local_width)
        .astype(jnp.bfloat16)
    )
    partial_out = jnp.dot(attended, output_weight, preferred_element_type=jnp.float32)
    resid = lax.psum(partial_out, "tensor") + output_bias
    hidden_state = source + resid
    second_low = layer_norm(hidden_state, second_gain, second_shift).astype(jnp.bfloat16)
    pre_act = jnp.dot(second_low, expand_weight, preferred_element_type=jnp.float32) + expand_bias
    activ_low = gelu_exact(pre_act).astype(jnp.bfloat16)
    partial_mlp = jnp.dot(activ_low, shrink_weight, preferred_element_type=jnp.float32)
    outputs = (
        hidden_state
        + lax.psum(partial_mlp.astype(jnp.bfloat16), "tensor").astype(jnp.float32)
        + shrink_bias
    ).astype(jnp.bfloat16)
    act_grad = jnp.einsum("td,fd->tf", cotangent, shrink_weight, preferred_element_type=jnp.float32)
    _, gelu_pull = jax.vjp(gelu_exact, pre_act)
    pre_grad = gelu_pull(act_grad)[0].astype(jnp.bfloat16)
    shrink_weight_grad = jnp.einsum(
        "tf,td->fd", activ_low, cotangent, preferred_element_type=jnp.float32
    )
    shrink_bias_grad = jnp.sum(upstream, axis=0)
    expand_weight_grad = jnp.einsum(
        "td,tf->df", second_low, pre_grad, preferred_element_type=jnp.float32
    )
    expand_bias_grad = jnp.sum(pre_grad.astype(jnp.float32), axis=0)
    second_part = jnp.einsum(
        "tf,df->td", pre_grad, expand_weight, preferred_element_type=jnp.float32
    )
    second_grad = lax.psum(second_part, "tensor")
    hidden_grad, second_gain_grad, second_shift_grad = norm_backward(
        hidden_state, second_gain, second_shift, second_grad
    )
    hidden_grad = hidden_grad + upstream
    resid_low = hidden_grad.astype(jnp.bfloat16)
    output_weight_grad = jnp.einsum(
        "tc,td->cd", attended, resid_low, preferred_element_type=jnp.float32
    )
    output_bias_grad = jnp.sum(resid_low.astype(jnp.float32), axis=0)
    attended_grad = (
        jnp.einsum("td,cd->tc", resid_low, output_weight, preferred_element_type=jnp.float32)
        .astype(jnp.bfloat16)
        .reshape(length, local_heads, HD)
    )
    probs = jnp.exp(biased_scores(query, keys, blocks, first_head) - logsum)
    probs_low = probs.astype(jnp.bfloat16)
    prob_grad = jnp.einsum("qhd,khd->hqk", attended_grad, vals, preferred_element_type=jnp.float32)
    vals_grad = jnp.einsum(
        "hqk,qhd->khd", probs_low, attended_grad, preferred_element_type=jnp.float32
    ).astype(jnp.bfloat16)
    row_delta = jnp.sum(probs * prob_grad, axis=-1, keepdims=True)
    score_grad = (probs * (prob_grad - row_delta)).astype(jnp.bfloat16)
    scale_factor = 1.0 / math.sqrt(HD)
    query_grad = (
        jnp.einsum("hqk,khd->qhd", score_grad, keys, preferred_element_type=jnp.float32)
        * scale_factor
    ).astype(jnp.bfloat16)
    keys_grad = (
        jnp.einsum("hqk,qhd->khd", score_grad, query, preferred_element_type=jnp.float32)
        * scale_factor
    ).astype(jnp.bfloat16)
    mixed_grad = jnp.stack([query_grad, keys_grad, vals_grad], axis=1).reshape(
        length, 3 * local_width
    )
    mixing_weight_grad = jnp.einsum(
        "td,tc->dc", normed_low, mixed_grad, preferred_element_type=jnp.float32
    ).reshape(width, 3, local_width)
    mixing_bias_grad = jnp.stack(
        [
            jnp.sum(query_grad.astype(jnp.float32), axis=0).reshape(local_width),
            jnp.sum(vals_grad.astype(jnp.float32), axis=0).reshape(local_width),
        ]
    )
    normed_part = jnp.einsum(
        "tc,dc->td", mixed_grad, flat_weight, preferred_element_type=jnp.float32
    )
    normed_grad = lax.psum(normed_part, "tensor")
    source_grad, first_gain_grad, first_shift_grad = norm_backward(
        source, first_gain, first_shift, normed_grad
    )
    input_grad = (source_grad + hidden_grad).astype(jnp.bfloat16)
    summed = lax.psum(
        (
            first_gain_grad,
            first_shift_grad,
            mixing_weight_grad,
            mixing_bias_grad,
            output_weight_grad,
            output_bias_grad,
            second_gain_grad,
            second_shift_grad,
            expand_weight_grad,
            expand_bias_grad,
            shrink_weight_grad,
            shrink_bias_grad,
        ),
        "dp",
    )
    return (
        outputs,
        input_grad,
        summed[0],
        summed[1],
        summed[2],
        summed[3],
        summed[4],
        summed[5],
        summed[6],
        summed[7],
        summed[8],
        summed[9],
        summed[10],
        summed[11],
    )


def solution(mesh):
    in_specs = (
        P("dp", None),
        P("dp", None),
        P(),
        P(),
        P(None, None, "tensor"),
        P(None, "tensor"),
        P("tensor", None),
        P(),
        P(),
        P(),
        P(None, "tensor"),
        P("tensor"),
        P("tensor", None),
        P(),
        P("dp", None),
    )
    out_specs = (
        P("dp", None),
        P("dp", None),
        P(),
        P(),
        P(None, None, "tensor"),
        P(None, "tensor"),
        P("tensor", None),
        P(),
        P(),
        P(),
        P(None, "tensor"),
        P("tensor"),
        P("tensor", None),
        P(),
    )
    return jax.shard_map(
        on_device, mesh=mesh, in_specs=in_specs, out_specs=out_specs, check_vma=False
    )
```

profile of v0, /device:TPU:0, one launch (start us, length us, event | category | flops | bytes accessed | tf_op | source)
XLA Modules:
  0.0 1608.9 jit_solution(12495282931637150068)
XLA Ops:
  13.2 8.8 copy.34
  22.0 8.5 fusion.13
  33.1 11.5 fusion.48
  44.6 8.9 exponential_reduce_fusion
  53.5 9.8 fusion.26
  68.8 225.7 %all-reduce.8.cloned.1.call-done = f32[768,2048]{1,0:T(8,128)} async-done(((f32[768,2048]{1,0:T(8,128)}), f32[768,2048]{1,0:T(8,128)}) %all-reduce.8.cloned.1.call-update) | async-done | bytes 6291472 | tf_op jit(solution)/shard_map/psum | solution.py:84
  294.5 4.6 fusion.46
  299.9 11.6 fusion.41
  311.5 26.1 %convert_reduce_fusion.2 = (f32[2048]{0:T(1024)}, bf16[768,2048]{1,0:T(8,128)(2,1)S(1)}, f32[768,2048]{1,0:T(8,128)}) fusion(f32[768,2048]{1,0:T(8,128)S(1)} %fusion.41, f32[2048]{0:T(1024)S(1)} %copy-done.37, bf16[768,2048]{1,0:T(8,128)(2,1)S(1)} %copy-done.9, bf16[2048,2048]{1,0:T(8,128)(2,1)} %param.27), kind=kOutput, calls=%fused_computation.28 | convolution fusion | flops 6560413696 | bytes 27279360 | tf_op jit(solution)/shard_map/td,fd->tf/dot_general | solution.py:95
  339.3 10.9 fusion.50
  350.5 6.6 multiply_convert_fusion.1
  358.8 10.2 convolution_convert_fusion
  369.1 203.1 %all-reduce.12.cloned.1.call-done = f32[768,2048]{1,0:T(8,128)} async-done(((f32[768,2048]{1,0:T(8,128)}), f32[768,2048]{1,0:T(8,128)}) %all-reduce.12.cloned.1.call-update) | async-done | bytes 6291472 | tf_op jit(solution)/shard_map/psum | solution.py:109
  572.2 5.8 multiply_reduce_fusion.1
  578.0 117.2 %all-reduce.10.cloned.1.call-done = bf16[768,2048]{1,0:T(8,128)(2,1)} async-done(((bf16[768,2048]{1,0:T(8,128)(2,1)}), bf16[768,2048]{1,0:T(8,128)(2,1)}) %all-reduce.10.cloned.1.call-update) | async-done | bytes 3145744 | tf_op jit(solution)/shard_map/psum | solution.py:92
  695.2 8.1 fusion.45
  707.8 9.6 convert_reduce_fusion.4
  717.4 11.9 multiply_reduce_fusion
  729.3 13.7 multiply_convert_fusion
  749.5 7.1 fusion.51
  756.8 12.9 fusion.53
  769.7 14.0 fusion.40
  787.6 9.8 fusion.33
  797.6 181.1 %all-reduce.14.cloned.1.call-done = f32[768,2048]{1,0:T(8,128)} async-done(((f32[768,2048]{1,0:T(8,128)}), f32[768,2048]{1,0:T(8,128)}) %all-reduce.14.cloned.1.call-update) | async-done | bytes 6291472 | tf_op jit(solution)/shard_map/psum | solution.py:156
  978.7 4.8 fusion.42
  984.2 4.6 fusion.9
  988.9 6.6 convert_reduce_fusion.1
  995.5 27.8 %all-reduce = (f32[2048]{0:T(1024)}, f32[2048]{0:T(1024)}, f32[2,512]{1,0:T(2,128)}, f32[2048]{0:T(1024)}, f32[2048]{0:T(1024)}, /*index=5*/f32[2048]{0:T(1024)}, f32[2048]{0:T(1024)}, f32[2048]{0:T(1024)}) all-reduce(f32[2048]{0:T(1024)S(1)} %get-tuple-element.16, ...), channel_id=1, replica_groups=mesh['dp'=8,'tensor'=4] {'dp'}, use_global_device_ids=true, to_apply=%region_16.17 | all-reduce | flops 15360 | bytes 122880 | tf_op jit(solution)/shard_map/psum | solution.py:161
  1023.4 543.2 %all-reduce.16.cloned.1.call-done = (f32[2048,3,512]{2,0,1:T(8,128)}, f32[512,2048]{1,0:T(8,128)}, f32[2048,2048]{1,0:T(8,128)}, f32[2048,2048]{1,0:T(8,128)}) async-done(((f32[2048,3,512]{2,0,1:T(8,128)}, f32[512,2048]{1,0:T(8,128)}, f32[2048,2048]{1,0:T(8,128)}, f32[2048,2048]{1,0:T(8,128)}), (f32[2048,3,512]{2,0,1:T(8,128)}, f32[512,2048]{1,0:T(8,128)}, f32[2048,2048]{1,0:T(8,128)}, ...) | async-done | bytes 50331664 | tf_op jit(solution)/shard_map/psum | solution.py:161
  1566.6 11.1 copy.54
  1579.8 14.0 copy.56
  1595.9 6.3 copy.57
  (154 shorter events, 38.3 us)
Async XLA Ops:
  7.2 57.0 %copy-start = (bf16[512,2048]{1,0:T(8,128)(2,1)S(1)}, bf16[512,2048]{1,0:T(8,128)(2,1)}, u32[]{:S(2)}) copy-start(bf16[512,2048]{1,0:T(8,128)(2,1)} %param.21) | copy-start | bytes 6291460
  7.2 287.3 %all-reduce.8.cloned.1.call-start = ((), (), s32[]{:S(2)}) async-start(), calls=%async_computation | async-start | bytes 12582912 | tf_op jit(solution)/shard_map/psum | solution.py:84
  11.6 10.4 copy-start.24
  13.1 8.8 copy-start.45
  30.6 14.0 copy-start.15
  32.6 20.9 %copy-start.30 = (f32[8,64]{1,0:T(8,128)}, f32[8,64]{1,0:T(8,128)S(1)}, u32[]{:S(2)}) copy-start(f32[8,64]{1,0:T(8,128)S(1)} %add.163) | copy-start | bytes 6148
  32.7 11.9 copy-start.35
  64.2 230.3 %copy-start.38 = (f32[2048]{0:T(1024)S(1)}, f32[2048]{0:T(1024)}, u32[]{:S(2)}) copy-start(f32[2048]{0:T(1024)} %param.22) | copy-start | bytes 24580
  68.8 503.4 %all-reduce.12.cloned.1.call-start = ((), (), s32[]{:S(2)}) async-start(), calls=%async_computation.2 | async-start | bytes 12582912 | tf_op jit(solution)/shard_map/psum | solution.py:109
  299.1 12.4 copy-start.5
  299.9 11.6 copy-start.9
  299.9 11.6 copy-start.37
  311.5 26.1 %copy-start.12 = (f32[768,2048]{1,0:T(8,128)}, f32[768,2048]{1,0:T(8,128)S(1)}, u32[]{:S(2)}) copy-start(f32[768,2048]{1,0:T(8,128)S(1)} %fusion.41) | copy-start | bytes 18874372
  350.3 345.0 %all-reduce.10.cloned.1.call-start = ((), (), s32[]{:S(2)}) async-start(), calls=%async_computation.1 | async-start | bytes 6291456 | tf_op jit(solution)/shard_map/psum | solution.py:92
  369.0 326.2 %copy-start.39 = (f32[2048]{0:T(1024)S(1)}, f32[2048]{0:T(1024)}, u32[]{:S(2)}) copy-start(f32[2048]{0:T(1024)} %param.28) | copy-start | bytes 24580
  369.0 609.6 %all-reduce.14.cloned.1.call-start = ((), (), s32[]{:S(2)}) async-start(), calls=%async_computation.3 | async-start | bytes 12582912 | tf_op jit(solution)/shard_map/psum | solution.py:156
  705.9 11.4 copy-start.20
  707.8 9.6 copy-start.8
  707.8 9.6 copy-start.31
  729.3 13.7 copy-start.13
  729.3 13.7 copy-start.36
  756.7 13.0 copy-start.44
  756.7 809.9 %all-reduce.16.cloned.1.call-start = ((), (), s32[]{:S(2)}) async-start(), calls=%async_computation.4 | async-start | bytes 100663296 | tf_op jit(solution)/shard_map/psum | solution.py:161
  756.8 12.9 copy-start.48
  769.7 14.0 copy-start.18
  769.7 14.0 copy-start.21
  797.4 186.2 %copy-start.33 = (f32[768]{0:T(1024)S(1)}, f32[768]{0:T(1024)}, u32[]{:S(2)}) copy-start(f32[768]{0:T(1024)} %copy-done.32) | copy-start | bytes 9220
  1566.6 11.1 copy-start.14
  1577.7 16.2 %slice-start = ((s8[16777216]{0:T(1024)(128)(4,1)}), s8[4194304]{0:T(1024)(128)(4,1)S(1)}, s32[]{:S(2)}) async-start(s8[16777216]{0:T(1024)(128)(4,1)} %bitcast.61), calls=%async_computation.5 | async-start | bytes 8388608
  1579.8 14.0 slice-start.1
  1579.8 14.0 slice-start.2
  1579.8 16.0 slice-start.3
  (28 other events, 110.1 us)
Sparse Core Ops, SparseCore 0:
  68.9 225.5 all-reduce.7
  350.4 221.7 all-reduce.11
  575.2 120.0 all-reduce.9
  756.8 221.8 all-reduce.13
  983.9 582.6 all-reduce.15
where the time goes:
time: 1620 us; the launch traced here: 1610 us
  waiting for transfers between devices  1270 us (78%)
  matrix products  169 us (10%)
  other arithmetic  71.5 us (4%)
  local copies, waits for them, and re-layouts  55.2 us (3%)
  blocking collectives  27.8 us (2%)
    psum x1, waiting for transfers between devices, on_device(): lax.psum((first_gain_grad, first_shift_grad, mixing_weight_grad, mixing_b...  543 us
    psum x1, waiting for transfers between devices, on_device(): resid = lax.psum(partial_out, 'tensor') + output_bias  226 us
    psum x1, waiting for transfers between devices, on_device(): second_grad = lax.psum(second_part, 'tensor')  203 us
    psum x1, waiting for transfers between devices, on_device(): normed_grad = lax.psum(normed_part, 'tensor')  181 us
    psum x1, waiting for transfers between devices, on_device(): lax.psum(partial_mlp.astype(jnp.bfloat16), 'tensor').astype(jnp.float32)  117 us
    unnamed x115, local copies, waits for them, and re-layouts  53 us
  transfers between devices with their start and end apart: 5, of which 5 were waited for; matrix products, arithmetic and copies ran while one was open for 5% of the time, Pallas kernels for 0%

commit v1 on v0

--- a/solution.py
+++ b/solution.py
@@ -106,7 +106,11 @@
     second_part = jnp.einsum(
         "tf,df->td", pre_grad, expand_weight, preferred_element_type=jnp.float32
     )
-    second_grad = lax.psum(second_part, "tensor")
+    second_grad = second_part
+    for hop in (1, 2):
+        second_grad = second_grad + lax.ppermute(
+            second_grad, "tensor", [(dev, dev ^ hop) for dev in range(4)]
+        )
     hidden_grad, second_gain_grad, second_shift_grad = norm_backward(
         hidden_state, second_gain, second_shift, second_grad
     )

time: 1620 us -> 1800 us (1.11)
  waiting for transfers between devices: 1270 us -> 1450 us
    ppermute x0 -> x2, waiting for transfers between devices: none -> 496 us  [on_device(): lax.ppermute(second_grad, 'tensor', [(dev, dev ^ hop) for dev in range(4)])]
    psum x1 -> x0, waiting for transfers between devices: 203 us -> none  [on_device(): second_grad = lax.psum(second_part, 'tensor')]
    psum x1, waiting for transfers between devices: 117 us -> 0.02 us  [on_device(): lax.psum(partial_mlp.astype(jnp.bfloat16), 'tensor').astype(jnp.float32)]
    unnamed x115 -> x119, local copies, waits for them, and re-layouts: 53 us -> 54 us
  transfers between devices with their start and end apart: 5 -> 6, of which waited for: 5 -> 5; matrix products, arithmetic and copies ran while one was open for 5% -> 4% of each run, Pallas kernels for 0% -> 0%
where the time goes in v1:
time: 1800 us; the launch traced here: 1790 us
  waiting for transfers between devices  1450 us (81%)
  matrix products  166 us (9%)
  other arithmetic  80.2 us (4%)
  local copies, waits for them, and re-layouts  56.3 us (3%)
  blocking collectives  27.8 us (2%)
    psum x1, waiting for transfers between devices, on_device(): lax.psum((first_gain_grad, first_shift_grad, mixing_weight_grad, mixing_b...  543 us
    ppermute x2, waiting for transfers between devices, on_device(): lax.ppermute(second_grad, 'tensor', [(dev, dev ^ hop) for dev in range(4)])  496 us
    psum x1, waiting for transfers between devices, on_device(): resid = lax.psum(partial_out, 'tensor') + output_bias  226 us
    psum x1, waiting for transfers between devices, on_device(): normed_grad = lax.psum(normed_part, 'tensor')  181 us
    unnamed x119, local copies, waits for them, and re-layouts  54 us
  transfers between devices with their start and end apart: 6, of which 5 were waited for; matrix products, arithmetic and copies ran while one was open for 4% of the time, Pallas kernels for 0%

profile of v1, /device:TPU:0, one launch (start us, length us, event | category | flops | bytes accessed | tf_op | source)
XLA Modules:
  0.0 1793.0 jit_solution(2444355581585543931)
XLA Ops:
  13.2 8.8 copy.34
  22.0 8.5 fusion.13
  33.1 11.5 fusion.48
  44.6 8.9 exponential_reduce_fusion
  53.5 9.9 fusion.26
  68.9 225.7 %all-reduce.7.cloned.1.call-done = f32[768,2048]{1,0:T(8,128)} async-done(((f32[768,2048]{1,0:T(8,128)}), f32[768,2048]{1,0:T(8,128)}) %all-reduce.7.cloned.1.call-update) | async-done | bytes 6291472 | tf_op jit(solution)/shard_map/psum | solution.py:84
  294.6 4.6 fusion.46
  300.0 11.6 fusion.41
  311.6 23.3 %convert_reduce_fusion.2 = (f32[2048]{0:T(1024)}, bf16[768,2048]{1,0:T(8,128)(2,1)S(1)}, f32[768,2048]{1,0:T(8,128)S(1)}) fusion(f32[768,2048]{1,0:T(8,128)S(1)} %fusion.41, f32[2048]{0:T(1024)S(1)} %copy-done.39, bf16[768,2048]{1,0:T(8,128)(2,1)S(1)} %copy-done.9, bf16[2048,2048]{1,0:T(8,128)(2,1)} %param.27), kind=kOutput, calls=%fused_computation.28 | convolution fusion | flops 6560413696 | bytes 27279360 | tf_op jit(solution)/shard_map/td,fd->tf/dot_general | solution.py:95
  334.9 10.2 fusion.50
  347.9 137.4 %collective-permute-done = f32[768,2048]{1,0:T(8,128)} collective-permute-done((f32[768,2048]{1,0:T(8,128)S(1)}, f32[768,2048]{1,0:T(8,128)}, u32[]{:S(2)}, u32[]{:S(2)}) %collective-permute-start) | collective-permute-done | bytes 6291488 | tf_op jit(solution)/shard_map/ppermute | solution.py:111
  485.2 9.2 add.189
  499.1 10.4 convolution_convert_fusion
  509.6 359.1 %collective-permute-done.1 = f32[768,2048]{1,0:T(8,128)} collective-permute-done((f32[768,2048]{1,0:T(8,128)}, f32[768,2048]{1,0:T(8,128)}, u32[]{:S(2)}, u32[]{:S(2)}) %collective-permute-start.1) | collective-permute-done | bytes 6291488 | tf_op jit(solution)/shard_map/ppermute | solution.py:111
  868.7 10.2 multiply_reduce_fusion.1
  879.0 8.1 fusion.45
  891.6 9.6 convert_reduce_fusion.4
  901.2 11.9 multiply_reduce_fusion
  913.1 13.7 multiply_convert_fusion
  933.4 7.1 fusion.51
  940.6 12.9 fusion.53
  953.5 14.0 fusion.40
  971.4 9.8 fusion.33
  981.4 181.5 %all-reduce.11.cloned.1.call-done = f32[768,2048]{1,0:T(8,128)} async-done(((f32[768,2048]{1,0:T(8,128)}), f32[768,2048]{1,0:T(8,128)}) %all-reduce.11.cloned.1.call-update) | async-done | bytes 6291472 | tf_op jit(solution)/shard_map/psum | solution.py:160
  1162.8 4.8 fusion.42
  1168.4 4.6 fusion.9
  1173.1 6.6 convert_reduce_fusion.1
  1179.7 27.8 %all-reduce = (f32[2048]{0:T(1024)}, f32[2048]{0:T(1024)}, f32[2,512]{1,0:T(2,128)}, f32[2048]{0:T(1024)}, f32[2048]{0:T(1024)}, /*index=5*/f32[2048]{0:T(1024)}, f32[2048]{0:T(1024)}, f32[2048]{0:T(1024)}) all-reduce(f32[2048]{0:T(1024)S(1)} %get-tuple-element.16, ...), channel_id=1, replica_groups=mesh['dp'=8,'tensor'=4] {'dp'}, use_global_device_ids=true, to_apply=%region_15.16 | all-reduce | flops 15360 | bytes 122880 | tf_op jit(solution)/shard_map/psum | solution.py:165
  1207.5 543.2 %all-reduce.13.cloned.1.call-done = (f32[2048,3,512]{2,0,1:T(8,128)}, f32[512,2048]{1,0:T(8,128)}, f32[2048,2048]{1,0:T(8,128)}, f32[2048,2048]{1,0:T(8,128)}) async-done(((f32[2048,3,512]{2,0,1:T(8,128)}, f32[512,2048]{1,0:T(8,128)}, f32[2048,2048]{1,0:T(8,128)}, f32[2048,2048]{1,0:T(8,128)}), (f32[2048,3,512]{2,0,1:T(8,128)}, f32[512,2048]{1,0:T(8,128)}, f32[2048,2048]{1,0:T(8,128)}, ...) | async-done | bytes 50331664 | tf_op jit(solution)/shard_map/psum | solution.py:165
  1750.8 11.1 copy.53
  1764.0 14.0 copy.55
  1780.0 6.3 copy.56
  (160 shorter events, 42.1 us)
Async XLA Ops:
  7.2 57.1 %copy-start = (bf16[512,2048]{1,0:T(8,128)(2,1)S(1)}, bf16[512,2048]{1,0:T(8,128)(2,1)}, u32[]{:S(2)}) copy-start(bf16[512,2048]{1,0:T(8,128)(2,1)} %param.21) | copy-start | bytes 6291460
  7.2 287.4 %all-reduce.7.cloned.1.call-start = ((), (), s32[]{:S(2)}) async-start(), calls=%async_computation | async-start | bytes 12582912 | tf_op jit(solution)/shard_map/psum | solution.py:84
  11.6 10.4 copy-start.26
  30.6 14.0 copy-start.15
  32.6 20.9 %copy-start.32 = (f32[8,64]{1,0:T(8,128)}, f32[8,64]{1,0:T(8,128)S(1)}, u32[]{:S(2)}) copy-start(f32[8,64]{1,0:T(8,128)S(1)} %add.167) | copy-start | bytes 6148
  32.7 11.9 copy-start.37
  53.5 9.9 copy-start.24
  64.3 230.3 %copy-start.40 = (f32[2048]{0:T(1024)S(1)}, f32[2048]{0:T(1024)}, u32[]{:S(2)}) copy-start(f32[2048]{0:T(1024)} %param.22) | copy-start | bytes 24580
  68.9 810.1 %all-reduce.9.cloned.1.call-start = ((), (), s32[]{:S(2)}) async-start(), calls=%async_computation.1 | async-start | bytes 6291456 | tf_op jit(solution)/shard_map/psum | solution.py:92
  299.2 12.5 copy-start.5
  300.0 11.6 copy-start.9
  300.0 11.6 copy-start.39
  334.9 10.2 copy-start.49
  347.9 137.4 %collective-permute-start = (f32[768,2048]{1,0:T(8,128)S(1)}, f32[768,2048]{1,0:T(8,128)}, u32[]{:S(2)}, u32[]{:S(2)}) collective-permute-start(f32[768,2048]{1,0:T(8,128)S(1)} %fusion.50), channel_id=1, source_target_pairs={{0,1},{1,0},{2,3},{3,2},{4,5},{5,4},{6,7},{7,6},{8,9},{9,8},{10,11... | collective-permute-start | bytes 18874376 | tf_op jit(solution)/shard_map/ppermute | solution.py:111
  494.5 374.2 %collective-permute-start.1 = (f32[768,2048]{1,0:T(8,128)}, f32[768,2048]{1,0:T(8,128)}, u32[]{:S(2)}, u32[]{:S(2)}) collective-permute-start(f32[768,2048]{1,0:T(8,128)} %add.189), channel_id=1, source_target_pairs={{0,2},{1,3},{2,0},{3,1},{4,6},{5,7},{6,4},{7,5},{8,10},{9,11},{10,... | collective-permute-start | bytes 18874376 | tf_op jit(solution)/shard_map/ppermute | solution.py:111
  509.5 369.5 %copy-start.41 = (f32[2048]{0:T(1024)S(1)}, f32[2048]{0:T(1024)}, u32[]{:S(2)}) copy-start(f32[2048]{0:T(1024)} %param.28) | copy-start | bytes 24580
  509.5 653.3 %all-reduce.11.cloned.1.call-start = ((), (), s32[]{:S(2)}) async-start(), calls=%async_computation.2 | async-start | bytes 12582912 | tf_op jit(solution)/shard_map/psum | solution.py:160
  889.7 11.4 copy-start.20
  891.6 9.6 copy-start.8
  913.1 13.7 copy-start.13
  913.1 13.7 copy-start.38
  940.5 13.0 copy-start.46
  940.5 810.2 %all-reduce.13.cloned.1.call-start = ((), (), s32[]{:S(2)}) async-start(), calls=%async_computation.3 | async-start | bytes 100663296 | tf_op jit(solution)/shard_map/psum | solution.py:165
  940.6 12.9 copy-start.50
  953.5 14.0 copy-start.18
  953.5 14.0 copy-start.21
  981.2 186.5 %copy-start.35 = (f32[768]{0:T(1024)S(1)}, f32[768]{0:T(1024)}, u32[]{:S(2)}) copy-start(f32[768]{0:T(1024)} %copy-done.34) | copy-start | bytes 9220
  1750.8 11.1 copy-start.14
  1761.8 16.2 slice-start
  1763.9 14.0 slice-start.1
  1764.0 14.0 slice-start.2
  1764.0 16.0 slice-start.3
  (31 other events, 131.5 us)
Sparse Core Ops, SparseCore 0:
  69.0 225.5 all-reduce.6
  509.6 286.1 all-reduce.8
  940.6 222.1 all-reduce.10
  1168.1 582.6 all-reduce.12
